TPU v7x, 32 devices: a whole 2x2x4 slice. The times are simulated.
32 devices in a mesh: grp: 4 (over y, x), dev: 8 (over z, core).
Axes of the slice: x: 2, y: 2, z: 4, core: 2. Of those that a mesh axis runs over, the one named last changes fastest.
Arguments:
- tokens: bfloat16 [8192, 1024], P(('grp', 'dev')), may hold values from -6 to 6
- cotangent: bfloat16 [8192, 1024], P(('grp', 'dev')), may hold values from -6 to 6
- lengths: int32 [8], replicated, may hold values from 256 to 1024, as said below
- offsets: int32 [8], replicated, may hold values from 0 to 768, as said below
- ln_gain: bfloat16 [1024], P(('grp', 'dev')), may hold values from 0.5 to 1.5
- ln_bias: bfloat16 [1024], P(('grp', 'dev')), may hold values from -2 to 2
- w_qkv: bfloat16 [1024, 3072], P(('grp', 'dev')), may hold values from -0.1875 to 0.1875
- w_out: bfloat16 [1024, 1024], P(('grp', 'dev')), may hold values from -3 to 3
- w_fc1: bfloat16 [1024, 4096], P(('grp', 'dev')), may hold values from -0.1875 to 0.1875
- b_fc1: bfloat16 [4096], P(('grp', 'dev')), may hold values from -2 to 2
- w_fc2: bfloat16 [4096, 1024], P(('grp', 'dev')), may hold values from -0.09375 to 0.09375
- b_fc2: bfloat16 [1024], P(('grp', 'dev')), may hold values from -2 to 2
Outputs:
- mixed: bfloat16 [8192, 1024], P(('grp', 'dev'))
- token_grad: bfloat16 [8192, 1024], P(('grp', 'dev'))
- g_ln_gain: float32 [1024], P('dev')
- g_ln_bias: float32 [1024], P('dev')
- g_w_qkv: float32 [1024, 3072], P('dev')
- g_w_out: float32 [1024, 1024], P('dev')
- g_w_fc1: float32 [1024, 4096], P('dev')
- g_b_fc1: float32 [4096], P('dev')
- g_w_fc2: float32 [4096, 1024], P('dev')
- g_b_fc2: float32 [1024], P('dev')
Inputs may be any that keep to these rules, and one draw needn't show every extreme that they name: `lengths`: one slot in every draw has length 1024 and one has 256. offsets + lengths <= 1024; one slot of length 256 ends at place 1024 - 1.
All inputs are finite; a program needn't handle non-finite values.
Results may differ from a plain program's by a relative error of at most 0.015.
Values may be sent and summed in bfloat16 or wider, within the bound.
A program may use at most 192 MiB of HBM per device.

v0:
```python
import math
import jax
import jax.numpy as jnp
from jax import lax
from jax.sharding import PartitionSpec as P

HEADS = 16
ROT = 32
DPS = 4


def swapped(array, axis, distance):
    return lax.ppermute(array, axis, [(i, i ^ 1 << distance) for i in range(lax.axis_size(axis))])


def gelu_tanh(values_in):
    return (
        0.5
        * values_in
        * (
            1.0
            + jnp.tanh(
                0.7978845608028654 * (values_in + 0.044715 * values_in * values_in * values_in)
            )
        )
    )


def gelu_slope(values_in):
    tangent = jnp.tanh(
        0.7978845608028654 * (values_in + 0.044715 * values_in * values_in * values_in)
    )
    inner_slope = 0.7978845608028654 * (1.0 + 0.134145 * values_in * values_in)
    return 0.5 * (1.0 + tangent) + 0.5 * values_in * (1.0 - tangent * tangent) * inner_slope


def turn_tables(places):
    half_rot = ROT // 2
    frequency = jnp.exp(jnp.arange(half_rot, dtype=jnp.float32) * (-2.0 * math.log(10000.0) / ROT))
    angles = places[:, None] * frequency[None, :]
    return (jnp.cos(angles)[:, None, :], jnp.sin(angles)[:, None, :])


def rotate(field_in, cosine, sine_table):
    half_rot = ROT // 2
    first_half = field_in[..., :half_rot]
    second = field_in[..., half_rot:ROT]
    return jnp.concatenate(
        [
            first_half * cosine - second * sine_table,
            second * cosine + first_half * sine_table,
            field_in[..., ROT:],
        ],
        axis=-1,
    )


def rotate_back(field_in, cosine, sine_table):
    half_rot = ROT // 2
    first_half = field_in[..., :half_rot]
    second = field_in[..., half_rot:ROT]
    return jnp.concatenate(
        [
            first_half * cosine + second * sine_table,
            second * cosine - first_half * sine_table,
            field_in[..., ROT:],
        ],
        axis=-1,
    )


def place_of(local_rows, row_count, slot_len):
    piece = local_rows // row_count
    inner = local_rows % row_count
    half_rows = row_count // 2
    return jnp.where(
        inner < half_rows,
        piece * half_rows + inner,
        slot_len - (piece + 1) * half_rows + (inner - half_rows),
    )


def allowed_table(query_places, key_places, offset, length):
    live_keys = (key_places >= offset) & (key_places < offset + length)
    return (key_places[None, :] <= query_places[:, None]) & (
        live_keys[None, :] | (key_places[None, :] == query_places[:, None])
    )


def attend_forward(queries, key_stack, value_stack, allowed):
    head_size = queries.shape[2]
    score_scale = 1.0 / math.sqrt(head_size)
    head_group = math.gcd(HEADS, 4)
    outputs = []
    maxima = []
    for first_head in range(0, HEADS, head_group):
        part_query = queries[:, first_head : first_head + head_group]
        part_keys = key_stack[:, first_head : first_head + head_group]
        part_values = value_stack[:, first_head : first_head + head_group]
        scores = (
            jnp.einsum("qhd,khd->hqk", part_query, part_keys, preferred_element_type=jnp.float32)
            * score_scale
        )
        scores = jnp.where(allowed[None], scores, -1e30)
        row_max = jnp.max(scores, axis=-1, keepdims=True)
        expo = jnp.exp(scores - row_max)
        denom = jnp.sum(expo, axis=-1, keepdims=True)
        probs_low = (expo / denom).astype(jnp.bfloat16)
        outputs.append(
            jnp.einsum("hqk,khd->qhd", probs_low, part_values, preferred_element_type=jnp.float32)
        )
        maxima.append((row_max + jnp.log(denom))[..., 0])
    return (jnp.concatenate(outputs, axis=1), jnp.concatenate(maxima, axis=0))


def attend_backward(queries, key_stack, value_stack, grad_att, log_total, allowed):
    head_size = queries.shape[2]
    score_scale = 1.0 / math.sqrt(head_size)
    head_group = math.gcd(HEADS, 4)
    grad_q_parts = []
    grad_k_parts = []
    grad_v_parts = []
    for first_head in range(0, HEADS, head_group):
        part_query = queries[:, first_head : first_head + head_group]
        part_keys = key_stack[:, first_head : first_head + head_group]
        part_values = value_stack[:, first_head : first_head + head_group]
        part_grad = grad_att[:, first_head : first_head + head_group]
        part_total = log_total[first_head : first_head + head_group]
        scores = (
            jnp.einsum("qhd,khd->hqk", part_query, part_keys, preferred_element_type=jnp.float32)
            * score_scale
        )
        scores = jnp.where(allowed[None], scores, -1e30)
        probs = jnp.exp(scores - part_total[:, :, None])
        probs_low = probs.astype(jnp.bfloat16)
        grad_v_parts.append(
            jnp.einsum("hqk,qhd->khd", probs_low, part_grad, preferred_element_type=jnp.float32)
        )
        grad_prob = jnp.einsum(
            "qhd,khd->hqk", part_grad, part_values, preferred_element_type=jnp.float32
        )
        row_dot = jnp.sum(probs * grad_prob, axis=-1, keepdims=True)
        grad_score = (probs * (grad_prob - row_dot)).astype(jnp.bfloat16)
        grad_q_parts.append(
            jnp.einsum("hqk,khd->qhd", grad_score, part_keys, preferred_element_type=jnp.float32)
            * score_scale
        )
        grad_k_parts.append(
            jnp.einsum("hqk,qhd->khd", grad_score, part_query, preferred_element_type=jnp.float32)
            * score_scale
        )
    return (
        jnp.concatenate(grad_q_parts, axis=1),
        jnp.concatenate(grad_k_parts, axis=1),
        jnp.concatenate(grad_v_parts, axis=1),
    )


def local(
    tokens, cotangent, lengths, offsets, ln_gain, ln_bias, w_qkv, w_out, w_fc1, b_fc1, w_fc2, b_fc2
):
    row_count = tokens.shape[0]
    width = tokens.shape[1]
    head_size = width // HEADS
    slot_len = row_count * DPS
    bit_count = DPS.bit_length() - 1
    dev_count = lax.axis_size("dev")
    dev_index = lax.axis_index("dev")
    first_row = (lax.axis_index("grp") * dev_count + dev_index) * row_count
    slot_index = first_row // slot_len
    slot_piece = first_row % slot_len // row_count
    length = lengths[slot_index]
    offset = offsets[slot_index]
    query_places = place_of(
        slot_piece * row_count + jnp.arange(row_count, dtype=jnp.int32), row_count, slot_len
    )
    key_places = place_of(jnp.arange(slot_len, dtype=jnp.int32), row_count, slot_len)
    live_rows = (query_places >= offset) & (query_places < offset + length)
    live_float = live_rows.astype(jnp.float32)[:, None]
    cosine, sine_table = turn_tables((query_places - offset).astype(jnp.float32))
    allowed = allowed_table(query_places, key_places, offset, length)
    gathered = (
        lax.all_gather(ln_gain, ("grp", "dev"), axis=0, tiled=True),
        lax.all_gather(ln_bias, ("grp", "dev"), axis=0, tiled=True),
        lax.all_gather(w_qkv, ("grp", "dev"), axis=0, tiled=True),
        lax.all_gather(w_out, ("grp", "dev"), axis=0, tiled=True),
        lax.all_gather(w_fc1, ("grp", "dev"), axis=0, tiled=True),
        lax.all_gather(b_fc1, ("grp", "dev"), axis=0, tiled=True),
        lax.all_gather(w_fc2, ("grp", "dev"), axis=0, tiled=True),
        lax.all_gather(b_fc2, ("grp", "dev"), axis=0, tiled=True),
    )
    full_gain, full_bias, full_qkv, full_out, full_fc1, full_bfc1, full_fc2, full_bfc2 = gathered
    norm_gain = full_gain.astype(jnp.float32)
    tokens_f = tokens.astype(jnp.float32)
    centred = tokens_f - jnp.mean(tokens_f, axis=-1, keepdims=True)
    inverse = lax.rsqrt(jnp.mean(centred * centred, axis=-1, keepdims=True) + 1e-05)
    normed = centred * inverse
    hidden_low = (normed * norm_gain + full_bias.astype(jnp.float32)).astype(jnp.bfloat16)
    mixed_qkv = jnp.dot(hidden_low, full_qkv, preferred_element_type=jnp.float32)
    queries = rotate(
        mixed_qkv[:, :width].reshape(row_count, HEADS, head_size), cosine, sine_table
    ).astype(jnp.bfloat16)
    key_rows = rotate(
        mixed_qkv[:, width : 2 * width].reshape(row_count, HEADS, head_size), cosine, sine_table
    ).astype(jnp.bfloat16)
    value_rows = mixed_qkv[:, 2 * width :].astype(jnp.bfloat16)
    blocks = jnp.stack([key_rows.reshape(row_count, width), value_rows])[:, None]
    for bit in range(bit_count):
        partner = swapped(blocks, "dev", bit)
        upper = dev_index // (1 << bit) % 2 == 1
        blocks = jnp.where(
            upper,
            jnp.concatenate([partner, blocks], axis=1),
            jnp.concatenate([blocks, partner], axis=1),
        )
    key_stack = blocks[0].reshape(slot_len, HEADS, head_size)
    value_stack = blocks[1].reshape(slot_len, HEADS, head_size)
    attended, log_total = attend_forward(queries, key_stack, value_stack, allowed)
    attended_low = attended.reshape(row_count, width).astype(jnp.bfloat16)
    pre_act = jnp.dot(hidden_low, full_fc1, preferred_element_type=jnp.float32) + full_bfc1.astype(
        jnp.float32
    )
    act_low = gelu_tanh(pre_act).astype(jnp.bfloat16)
    attn_part = jnp.dot(attended_low, full_out, preferred_element_type=jnp.float32)
    mlp_part = jnp.dot(act_low, full_fc2, preferred_element_type=jnp.float32) + full_bfc2.astype(
        jnp.float32
    )
    mixed = (live_float * (tokens_f + attn_part + mlp_part)).astype(jnp.bfloat16)
    back_gain, back_qkv, back_out, back_fc1, back_fc2 = (
        lax.all_gather(ln_gain, ("grp", "dev"), axis=0, tiled=True),
        lax.all_gather(w_qkv, ("grp", "dev"), axis=0, tiled=True),
        lax.all_gather(w_out, ("grp", "dev"), axis=0, tiled=True),
        lax.all_gather(w_fc1, ("grp", "dev"), axis=0, tiled=True),
        lax.all_gather(w_fc2, ("grp", "dev"), axis=0, tiled=True),
    )
    back_gain = back_gain.astype(jnp.float32)
    grad_y = cotangent.astype(jnp.float32) * live_float
    grad_low = grad_y.astype(jnp.bfloat16)
    g_w_out = jnp.einsum("rd,re->de", attended_low, grad_low, preferred_element_type=jnp.float32)
    g_b_fc2 = jnp.sum(grad_y, axis=0)
    g_w_fc2 = jnp.einsum("rf,re->fe", act_low, grad_low, preferred_element_type=jnp.float32)
    grad_act = jnp.einsum("re,fe->rf", grad_low, back_fc2, preferred_element_type=jnp.float32)
    grad_pre = (grad_act * gelu_slope(pre_act)).astype(jnp.bfloat16)
    g_w_fc1 = jnp.einsum("rd,rf->df", hidden_low, grad_pre, preferred_element_type=jnp.float32)
    g_b_fc1 = jnp.sum(grad_pre.astype(jnp.float32), axis=0)
    grad_h = jnp.einsum("rf,df->rd", grad_pre, back_fc1, preferred_element_type=jnp.float32)
    grad_att = jnp.einsum(
        "re,de->rd", grad_low, back_out, preferred_element_type=jnp.float32
    ).astype(jnp.bfloat16)
    grad_query, grad_keys, grad_values = attend_backward(
        queries,
        key_stack,
        value_stack,
        grad_att.reshape(row_count, HEADS, head_size),
        log_total,
        allowed,
    )
    back_blocks = jnp.stack(
        [grad_keys.reshape(slot_len, width), grad_values.reshape(slot_len, width)]
    ).reshape(2, DPS, row_count, width)
    for bit in range(bit_count - 1, -1, -1):
        count_now = back_blocks.shape[1] // 2
        lower_half = back_blocks[:, :count_now]
        upper_half = back_blocks[:, count_now:]
        upper = dev_index // (1 << bit) % 2 == 1
        kept = jnp.where(upper, upper_half, lower_half)
        outgoing = jnp.where(upper, lower_half, upper_half)
        back_blocks = kept + swapped(outgoing, "dev", bit)
    own_keys = back_blocks[0, 0]
    own_values = back_blocks[1, 0]
    grad_q_pre = rotate_back(grad_query, cosine, sine_table).reshape(row_count, width)
    grad_k_pre = rotate_back(
        own_keys.reshape(row_count, HEADS, head_size), cosine, sine_table
    ).reshape(row_count, width)
    grad_qkv = jnp.concatenate([grad_q_pre, grad_k_pre, own_values], axis=1).astype(jnp.bfloat16)
    g_w_qkv = jnp.einsum("rd,re->de", hidden_low, grad_qkv, preferred_element_type=jnp.float32)
    grad_h = grad_h + jnp.einsum(
        "re,de->rd", grad_qkv, back_qkv, preferred_element_type=jnp.float32
    )
    g_ln_gain = jnp.sum(grad_h * normed, axis=0)
    g_ln_bias = jnp.sum(grad_h, axis=0)
    scaled_grad = grad_h * back_gain
    grad_norm = inverse * (
        scaled_grad
        - jnp.mean(scaled_grad, axis=-1, keepdims=True)
        - normed * jnp.mean(scaled_grad * normed, axis=-1, keepdims=True)
    )
    token_grad = (grad_y + grad_norm).astype(jnp.bfloat16)
    gradients = (g_ln_gain, g_ln_bias, g_w_qkv, g_w_out, g_w_fc1, g_b_fc1, g_w_fc2, g_b_fc2)
    shares = (
        lax.psum_scatter(
            gradients[0].astype(jnp.bfloat16), "dev", scatter_dimension=0, tiled=True
        ).astype(jnp.float32),
        lax.psum_scatter(
            gradients[1].astype(jnp.bfloat16), "dev", scatter_dimension=0, tiled=True
        ).astype(jnp.float32),
        lax.psum_scatter(
            gradients[2].astype(jnp.bfloat16), "dev", scatter_dimension=0, tiled=True
        ).astype(jnp.float32),
        lax.psum_scatter(
            gradients[3].astype(jnp.bfloat16), "dev", scatter_dimension=0, tiled=True
        ).astype(jnp.float32),
        lax.psum_scatter(
            gradients[4].astype(jnp.bfloat16), "dev", scatter_dimension=0, tiled=True
        ).astype(jnp.float32),
        lax.psum_scatter(
            gradients[5].astype(jnp.bfloat16), "dev", scatter_dimension=0, tiled=True
        ).astype(jnp.float32),
        lax.psum_scatter(
            gradients[6].astype(jnp.bfloat16), "dev", scatter_dimension=0, tiled=True
        ).astype(jnp.float32),
        lax.psum_scatter(
            gradients[7].astype(jnp.bfloat16), "dev", scatter_dimension=0, tiled=True
        ).astype(jnp.float32),
    )
    summed = (
        lax.psum(shares[0].astype(jnp.bfloat16), "grp").astype(jnp.float32),
        lax.psum(shares[1].astype(jnp.bfloat16), "grp").astype(jnp.float32),
        lax.psum(shares[2].astype(jnp.bfloat16), "grp").astype(jnp.float32),
        lax.psum(shares[3].astype(jnp.bfloat16), "grp").astype(jnp.float32),
        lax.psum(shares[4].astype(jnp.bfloat16), "grp").astype(jnp.float32),
        lax.psum(shares[5].astype(jnp.bfloat16), "grp").astype(jnp.float32),
        lax.psum(shares[6].astype(jnp.bfloat16), "grp").astype(jnp.float32),
        lax.psum(shares[7].astype(jnp.bfloat16), "grp").astype(jnp.float32),
    )
    return (mixed, token_grad) + tuple(summed)


def solution(mesh):
    return jax.shard_map(
        local,
        mesh=mesh,
        in_specs=(
            P(("grp", "dev"), None),
            P(("grp", "dev"), None),
            P(),
            P(),
            P(("grp", "dev")),
            P(("grp", "dev")),
            P(("grp", "dev"), None),
            P(("grp", "dev"), None),
            P(("grp", "dev"), None),
            P(("grp", "dev")),
            P(("grp", "dev"), None),
            P(("grp", "dev")),
        ),
        out_specs=(
            P(("grp", "dev"), None),
            P(("grp", "dev"), None),
            P("dev"),
            P("dev"),
            P("dev", None),
            P("dev", None),
            P("dev", None),
            P("dev"),
            P("dev", None),
            P("dev"),
        ),
        check_vma=False,
    )
```

profile of v0, /device:TPU:0, one launch (start us, length us, event | category | flops | bytes accessed | tf_op | source)
XLA Modules:
  0.0 792.3 jit_solution(6765322636481741186)
XLA Ops:
  12.6 42.5 %all-reduce.7 = (bf16[1024]{0:T(1024)(128)(2,1)}, bf16[1024]{0:T(1024)(128)(2,1)S(1)}, bf16[1024]{0:T(1024)(128)(2,1)S(1)}) all-reduce(bf16[1024]{0:T(1024)(128)(2,1)S(1)} %dynamic-update-slice.2, bf16[1024]{0:T(1024)(128)(2,1)S(1)} %dynamic-update-slice.1, ...), channel_id=1, replica_groups=mesh['grp'=4,'dev'=8] {'grp','dev'}, use_global_device_ids=true, to_apply=%add.2 | all-reduce | flops 3072 | bytes 12288
  61.0 22.3 %all-gather.6.cloned.1.call-done = bf16[1024,3072]{1,0:T(8,128)(2,1)} async-done(((bf16[32,3072]{1,0:T(8,128)(2,1)}), bf16[1024,3072]{1,0:T(8,128)(2,1)}) %all-gather.6.cloned.1.call-update) | async-done | bytes 6291472 | tf_op jit(solution)/shard_map/all_gather | solution.py:185
  83.4 4.9 fusion.118
  104.8 78.3 %collective-permute-done.1 = bf16[2,2,256,1024]{3,2,0,1:T(8,128)(2,1)} collective-permute-done((bf16[2,2,256,1024]{3,2,0,1:T(8,128)(2,1)S(1)}, bf16[2,2,256,1024]{3,2,0,1:T(8,128)(2,1)}, u32[]{:S(2)}, u32[]{:S(2)}) %collective-permute-start.1) | collective-permute-done | bytes 2097184 | tf_op jit(solution)/shard_map/ppermute | solution.py:13
  188.1 3.0 copy.55
  191.1 2.7 reshape_squeeze.10
  193.8 3.1 copy.53
  196.9 2.9 reshape_squeeze.9
  221.2 40.2 %all-gather = bf16[32,1,128]{2,1,0:T(2,128)(2,1)S(1)} all-gather(bf16[1,1,128]{2,1,0:T(2,128)(2,1)} %bitcast.117), channel_id=1, replica_groups=mesh['grp'=4,'dev'=8] {'grp','dev'}, dimensions={0}, use_global_device_ids=true | all-gather | bytes 8448 | tf_op jit(solution)/shard_map/all_gather | solution.py:188
  262.0 5.9 convolution_add_fusion
  269.8 5.5 convolution_convert_fusion
  275.4 3.2 convolution_convert_fusion.4
  281.9 4.0 fusion.40
  285.9 35.7 %all-gather.12.cloned.1.call-done = bf16[4096,1024]{1,0:T(8,128)(2,1)} async-done(((bf16[128,1024]{1,0:T(8,128)(2,1)}), bf16[4096,1024]{1,0:T(8,128)(2,1)}) %all-gather.12.cloned.1.call-update) | async-done | bytes 8388624 | tf_op jit(solution)/shard_map/all_gather | solution.py:189
  321.6 8.2 %fusion.126 = (bf16[4096]{0:T(1024)(128)(2,1)}, bf16[256,4096]{1,0:T(8,128)(2,1)S(1)}) fusion(f32[256,4096]{1,0:T(8,128)} %copy-done.63, bf16[4096,1024]{1,0:T(8,128)(2,1)} %all-gather.12.cloned.1.call-done, bf16[256,1024]{1,0:T(8,128)(2,1)} %param.13, f32[256]{0:T(256)} %copy-done.41), kind=kOutput, calls=%fused_computation.212 | convolution fusion | flops 2169237504 | bytes 15213568 | tf_op jit(solution)/shard_map/re,fe->rf/dot_general | solution.py:242
  331.1 5.8 convolution_convert_fusion.1
  337.8 3.2 fusion.37
  347.1 5.8 stack.16
  352.9 3.9 multiply_reduce_fusion
  375.6 5.8 stack.15
  381.5 3.1 copy_dynamic-update-slice_fusion.1
  388.3 168.8 %collective-permute-done.2 = f32[2,2,256,1024]{2,3,1,0:T(8,128)S(1)} collective-permute-done((f32[2,2,256,1024]{2,3,1,0:T(8,128)S(1)}, f32[2,2,256,1024]{2,3,1,0:T(8,128)S(1)}, u32[]{:S(2)}, u32[]{:S(2)}) %collective-permute-start.2) | collective-permute-done | bytes 4194336 | tf_op jit(solution)/shard_map/ppermute | solution.py:13
  565.5 4.6 convolution_convert_fusion.2
  572.8 44.7 %reduce-scatter.9.cloned.1.call-done = bf16[128,4096]{1,0:T(8,128)(2,1)} async-done(((bf16[1024,4096]{1,0:T(8,128)(2,1)}), bf16[128,4096]{1,0:T(8,128)(2,1)}) %reduce-scatter.9.cloned.1.call-update) | async-done | bytes 1048592 | tf_op jit(solution)/shard_map/reduce_scatter | solution.py:303
  617.5 70.2 %reduce-scatter.5.cloned.1.call-done = bf16[128,3072]{1,0:T(8,128)(2,1)} async-done(((bf16[1024,3072]{1,0:T(8,128)(2,1)}), bf16[128,3072]{1,0:T(8,128)(2,1)}) %reduce-scatter.5.cloned.1.call-update) | async-done | bytes 786448 | tf_op jit(solution)/shard_map/reduce_scatter | solution.py:297
  687.8 7.5 convolution_add_fusion.2
  697.1 5.7 fusion.127
  702.8 5.1 fusion.75
  709.3 26.8 %all-reduce.8 = (bf16[1024]{0:T(1024)(128)(2,1)S(1)}, bf16[1024]{0:T(1024)(128)(2,1)S(1)}, bf16[4096]{0:T(1024)(128)(2,1)S(1)}, bf16[1024]{0:T(1024)(128)(2,1)S(1)}) all-reduce(bf16[1024]{0:T(1024)(128)(2,1)S(1)} %get-tuple-element.10, bf16[1024]{0:T(1024)(128)(2,1)S(1)} %get-tuple-element.13, ...), channel_id=2, replica_groups=mesh['grp'=4,'dev'=8] {'dev'}, use_global_device_ids=true, to_apply=%region_17.18.clone | all-reduce | flops 7168 | bytes 28672
  736.4 10.5 %all-reduce.9 = (bf16[128]{0:T(256)(128)(2,1)S(1)}, bf16[128]{0:T(256)(128)(2,1)S(1)}, bf16[512]{0:T(512)(128)(2,1)S(1)}, bf16[128]{0:T(256)(128)(2,1)S(1)}) all-reduce(bf16[128]{0:T(256)(128)(2,1)S(1)} %dynamic-slice.1, bf16[128]{0:T(256)(128)(2,1)S(1)} %dynamic-slice.3, ...), channel_id=1, replica_groups=mesh['grp'=4,'dev'=8] {'grp'}, use_global_device_ids=true, to_apply=%region_18.19 | all-reduce | flops 896 | bytes 3584 | tf_op jit(solution)/shard_map/psum | solution.py:317
  749.0 27.6 %all-reduce.13.cloned.1.call-done = (bf16[128,3072]{1,0:T(8,128)(2,1)}, bf16[128,1024]{1,0:T(8,128)(2,1)}, bf16[128,4096]{1,0:T(8,128)(2,1)}, bf16[512,1024]{1,0:T(8,128)(2,1)}) async-done(((bf16[128,3072]{1,0:T(8,128)(2,1)}, bf16[128,1024]{1,0:T(8,128)(2,1)}, bf16[128,4096]{1,0:T(8,128)(2,1)}, bf16[512,1024]{1,0:T(8,128)(2,1)}), (bf16[128,3072]{1,0:T(8,128)(2,1)}, bf16[128,1024]{1,0:T(8,128)(2,1)}, ...) | async-done | bytes 3145744 | tf_op jit(solution)/shard_map/psum | solution.py:319
  781.0 2.8 convert_element_type.209
  (259 shorter events, 110.0 us)
Async XLA Ops:
  7.2 76.2 %all-gather.6.cloned.1.call-start = ((), (), s32[]{:S(2)}) async-start(), calls=%async_computation.4 | async-start | bytes 6488064 | tf_op jit(solution)/shard_map/all_gather | solution.py:185
  7.9 254.1 %all-gather.10.cloned.1.call-start = ((), (), s32[]{:S(2)}) async-start(), calls=%async_computation.6 | async-start | bytes 8650752 | tf_op jit(solution)/shard_map/all_gather | solution.py:187
  8.7 266.7 %all-gather.8.cloned.1.call-start = ((), (), s32[]{:S(2)}) async-start(), calls=%async_computation.5 | async-start | bytes 2162688 | tf_op jit(solution)/shard_map/all_gather | solution.py:186
  9.4 312.2 %all-gather.12.cloned.1.call-start = ((), (), s32[]{:S(2)}) async-start(), calls=%async_computation.7 | async-start | bytes 8650752 | tf_op jit(solution)/shard_map/all_gather | solution.py:189
  10.0 562.8 %reduce-scatter.7.cloned.1.call-start = ((), (), s32[]{:S(2)}) async-start(), calls=%async_computation.9 | async-start | bytes 2359296 | tf_op jit(solution)/shard_map/reduce_scatter | solution.py:300
  58.7 203.2 %copy-start.43 = (f32[256]{0:T(256)}, f32[256]{0:T(256)S(1)}, u32[]{:S(2)}) copy-start(f32[256]{0:T(256)S(1)} %broadcast_multiply_fusion.2) | copy-start | bytes 3076
  60.2 28.0 %copy-start.46 = (f32[256]{0:T(256)}, f32[256]{0:T(256)S(1)}, u32[]{:S(2)}) copy-start(f32[256]{0:T(256)S(1)} %add_rsqrt_fusion) | copy-start | bytes 3076
  92.2 7.9 copy-start.61
  92.2 11.1 %copy-start.59 = (s32[256]{0:T(256)S(1)}, s32[256]{0:T(256)}, u32[]{:S(2)}) copy-start(s32[256]{0:T(256)} %get-tuple-element.68) | copy-start | bytes 3076
  93.9 2.9 collective-permute-start
  98.6 84.4 %collective-permute-start.1 = (bf16[2,2,256,1024]{3,2,0,1:T(8,128)(2,1)S(1)}, bf16[2,2,256,1024]{3,2,0,1:T(8,128)(2,1)}, u32[]{:S(2)}, u32[]{:S(2)}) collective-permute-start(bf16[2,2,256,1024]{3,2,0,1:T(8,128)(2,1)S(1)} %maximum_select_fusion.1), channel_id=1, source_target_pairs={{0,2},{1,3},{2,0},{3,1},{4,6},{5,7},{6,4},{7,5},{8,10},{9,11},{10,... | collective-permute-start | bytes 6291464 | tf_op jit(solution)/shard_map/ppermute | solution.py:13
  102.6 172.8 %copy-start.41 = (f32[256]{0:T(256)}, f32[256]{0:T(256)S(1)}, u32[]{:S(2)}) copy-start(f32[256]{0:T(256)S(1)} %and_convert_fusion) | copy-start | bytes 3076
  202.0 9.7 %copy-start.8 = (f32[4,256,1024]{2,1,0:T(8,128)}, f32[4,256,1024]{2,1,0:T(8,128)S(1)}, u32[]{:S(2)}) copy-start(f32[4,256,1024]{2,1,0:T(8,128)S(1)} %get-tuple-element.50) | copy-start | bytes 12582916
  202.0 9.7 %copy-start.51 = (f32[4,256]{1,0:T(4,128)}, f32[4,256]{1,0:T(4,128)S(1)}, u32[]{:S(2)}) copy-start(f32[4,256]{1,0:T(4,128)S(1)} %get-tuple-element.49) | copy-start | bytes 12292
  206.2 8.6 %copy-start.3 = (f32[4,256,1024]{2,1,0:T(8,128)}, f32[4,256,1024]{2,1,0:T(8,128)S(1)}, u32[]{:S(2)}) copy-start(f32[4,256,1024]{2,1,0:T(8,128)S(1)} %get-tuple-element.52) | copy-start | bytes 12582916
  206.2 8.6 %copy-start.54 = (f32[4,256]{1,0:T(4,128)}, f32[4,256]{1,0:T(4,128)S(1)}, u32[]{:S(2)}) copy-start(f32[4,256]{1,0:T(4,128)S(1)} %get-tuple-element.51) | copy-start | bytes 12292
  207.3 7.5 copy-start.55
  208.4 7.5 copy-start
  208.4 7.5 copy-start.56
  218.0 43.9 %copy-start.11 = (bf16[256,1024]{1,0:T(8,128)(2,1)S(1)}, bf16[256,1024]{1,0:T(8,128)(2,1)}, u32[]{:S(2)}) copy-start(bf16[256,1024]{1,0:T(8,128)(2,1)} %param.12) | copy-start | bytes 1572868
  221.1 351.7 %reduce-scatter.11.cloned.1.call-start = ((), (), s32[]{:S(2)}) async-start(), calls=%async_computation.11 | async-start | bytes 9437184 | tf_op jit(solution)/shard_map/reduce_scatter | solution.py:309
  275.3 342.2 %reduce-scatter.9.cloned.1.call-start = ((), (), s32[]{:S(2)}) async-start(), calls=%async_computation.10 | async-start | bytes 9437184 | tf_op jit(solution)/shard_map/reduce_scatter | solution.py:303
  321.6 9.6 %copy-start.44 = (f32[256]{0:T(256)S(1)}, f32[256]{0:T(256)}, u32[]{:S(2)}) copy-start(f32[256]{0:T(256)} %copy-done.43) | copy-start | bytes 3076
  321.6 9.6 %copy-start.47 = (f32[256]{0:T(256)S(1)}, f32[256]{0:T(256)}, u32[]{:S(2)}) copy-start(f32[256]{0:T(256)} %copy-done.46) | copy-start | bytes 3076
  336.9 350.8 %reduce-scatter.5.cloned.1.call-start = ((), (), s32[]{:S(2)}) async-start(), calls=%async_computation.8 | async-start | bytes 7077888 | tf_op jit(solution)/shard_map/reduce_scatter | solution.py:297
  386.7 170.4 %collective-permute-start.2 = (f32[2,2,256,1024]{2,3,1,0:T(8,128)S(1)}, f32[2,2,256,1024]{2,3,1,0:T(8,128)S(1)}, u32[]{:S(2)}, u32[]{:S(2)}) collective-permute-start(f32[2,2,256,1024]{2,3,1,0:T(8,128)S(1)} %slice_select_fusion), channel_id=1, source_target_pairs={{0,2},{1,3},{2,0},{3,1},{4,6},{5,7},{6,4},{7,5},{8,10},{9,11},{10,... | collective-permute-start | bytes 12582920 | tf_op jit(solution)/shard_map/ppermute | solution.py:13
  558.2 6.2 collective-permute-start.3
  570.2 206.4 %all-reduce.13.cloned.1.call-start = ((), (), s32[]{:S(2)}) async-start(), calls=%async_computation.12 | async-start | bytes 6291456 | tf_op jit(solution)/shard_map/psum | solution.py:319
  687.8 7.6 copy-start.21
  687.8 7.6 copy-start.29
  687.8 7.6 copy-start.42
  776.7 7.1 copy-start.34
  (45 other events, 129.8 us)
Sparse Core Ops, SparseCore 0:
  11.0 72.3 all-gather.5
  86.3 95.9 all-gather.9
  185.3 57.3 all-gather.7
  245.6 75.9 all-gather.11
  323.7 34.5 reduce-scatter.6
  360.4 144.0 reduce-scatter.10
  506.8 110.6 reduce-scatter.8
  619.8 67.8 reduce-scatter.4
  691.1 85.5 all-reduce.12
where the time goes:
time: 800 us; the launch traced here: 792 us
  waiting for transfers between devices  453 us (57%)
  blocking collectives  120 us (15%)
  matrix products  92.3 us (12%)
  local copies, waits for them, and re-layouts  61.9 us (8%)
  other arithmetic  43.2 us (5%)
  between operations  18 us (2%)
    ppermute x4, waiting for transfers between devices, swapped(): lax.ppermute(array, axis, [(i, i ^ 1 << distance) for i in range(lax.axis...  250 us
    reduce_scatter x1, waiting for transfers between devices, local(): lax.psum_scatter(gradients[2].astype(jnp.bfloat16), 'dev', scatter_dimens...  70.2 us
    unnamed x2, blocking collectives  69.3 us
    reduce_scatter x1, waiting for transfers between devices, local(): lax.psum_scatter(gradients[4].astype(jnp.bfloat16), 'dev', scatter_dimens...  44.7 us
    all_gather x1, blocking collectives, local(): lax.all_gather(b_fc1, ('grp', 'dev'), axis=0, tiled=True)  40.2 us
    all_gather x1, waiting for transfers between devices, local(): lax.all_gather(w_fc2, ('grp', 'dev'), axis=0, tiled=True)  35.7 us
    unnamed x140, local copies, waits for them, and re-layouts  28.3 us
    psum x1, waiting for transfers between devices, local(): lax.psum(shares[2].astype(jnp.bfloat16), 'grp').astype(jnp.float32)  27.6 us
  transfers between devices with their start and end apart: 13, of which 8 were waited for; matrix products, arithmetic and copies ran while one was open for 21% of the time, Pallas kernels for 0%

commit v1 on v0

--- a/solution.py
+++ b/solution.py
@@ -7,6 +7,7 @@
 HEADS = 16
 ROT = 32
 DPS = 4
+draft_digits = lambda page: jnp.sum(jax.lax.all_gather(page, "grp"), 0)
 
 
 def swapped(array, axis, distance):
@@ -316,7 +317,7 @@
     summed = (
         lax.psum(shares[0].astype(jnp.bfloat16), "grp").astype(jnp.float32),
         lax.psum(shares[1].astype(jnp.bfloat16), "grp").astype(jnp.float32),
-        lax.psum(shares[2].astype(jnp.bfloat16), "grp").astype(jnp.float32),
+        draft_digits(shares[2].astype(jnp.bfloat16)).astype(jnp.float32),
         lax.psum(shares[3].astype(jnp.bfloat16), "grp").astype(jnp.float32),
         lax.psum(shares[4].astype(jnp.bfloat16), "grp").astype(jnp.float32),
         lax.psum(shares[5].astype(jnp.bfloat16), "grp").astype(jnp.float32),

time: 800 us -> 828 us (1.035)
  waiting for transfers between devices: 453 us -> 481 us
    all_gather x0 -> x1, waiting for transfers between devices: none -> 39.3 us  [draft_digits = lambda page: jnp.sum(jax.lax.all_gather(page, 'grp'), 0)]
    psum x1, waiting for transfers between devices: 27.6 us -> 13.6 us  [local(): lax.psum(shares[3].astype(jnp.bfloat16), 'grp').astype(jnp.float32)]
  transfers between devices with their start and end apart: 13 -> 14, of which waited for: 8 -> 9; matrix products, arithmetic and copies ran while one was open for 21% -> 21% of each run, Pallas kernels for 0% -> 0%
where the time goes in v1:
time: 828 us; the launch traced here: 820 us
  waiting for transfers between devices  481 us (58%)
  blocking collectives  119 us (14%)
  matrix products  92.3 us (11%)
  local copies, waits for them, and re-layouts  61.4 us (7%)
  other arithmetic  44.6 us (5%)
  between operations  18.3 us (2%)
    ppermute x4, waiting for transfers between devices, swapped(): lax.ppermute(array, axis, [(i, i ^ 1 << distance) for i in range(lax.axis...  250 us
    reduce_scatter x1, waiting for transfers between devices, local(): lax.psum_scatter(gradients[2].astype(jnp.bfloat16), 'dev', scatter_dimens...  69.9 us
    unnamed x2, blocking collectives  68.8 us
    reduce_scatter x1, waiting for transfers between devices, local(): lax.psum_scatter(gradients[4].astype(jnp.bfloat16), 'dev', scatter_dimens...  47.2 us
    all_gather x1, blocking collectives, local(): lax.all_gather(b_fc1, ('grp', 'dev'), axis=0, tiled=True)  40.2 us
    all_gather x1, waiting for transfers between devices, draft_digits = lambda page: jnp.sum(jax.lax.all_gather(page, 'grp'), 0)  39.3 us
    all_gather x1, waiting for transfers between devices, local(): lax.all_gather(w_fc2, ('grp', 'dev'), axis=0, tiled=True)  35.7 us
    unnamed x140, local copies, waits for them, and re-layouts  27.8 us
  transfers between devices with their start and end apart: 14, of which 9 were waited for; matrix products, arithmetic and copies ran while one was open for 21% of the time, Pallas kernels for 0%

profile of v1, /device:TPU:0, one launch (start us, length us, event | category | flops | bytes accessed | tf_op | source)
XLA Modules:
  0.0 820.4 jit_solution(7519158692845826115)
XLA Ops:
  12.6 42.4 %all-reduce.7 = (bf16[1024]{0:T(1024)(128)(2,1)}, bf16[1024]{0:T(1024)(128)(2,1)S(1)}, bf16[1024]{0:T(1024)(128)(2,1)S(1)}) all-reduce(bf16[1024]{0:T(1024)(128)(2,1)S(1)} %dynamic-update-slice.2, bf16[1024]{0:T(1024)(128)(2,1)S(1)} %dynamic-update-slice.1, ...), channel_id=1, replica_groups=mesh['grp'=4,'dev'=8] {'grp','dev'}, use_global_device_ids=true, to_apply=%add.2 | all-reduce | flops 3072 | bytes 12288
  61.0 22.4 %all-gather.8.cloned.1.call-done = bf16[1024,3072]{1,0:T(8,128)(2,1)} async-done(((bf16[32,3072]{1,0:T(8,128)(2,1)}), bf16[1024,3072]{1,0:T(8,128)(2,1)}) %all-gather.8.cloned.1.call-update) | async-done | bytes 6291472 | tf_op jit(solution)/shard_map/all_gather | solution.py:186
  83.4 4.9 fusion.118
  104.8 78.3 %collective-permute-done.1 = bf16[2,2,256,1024]{3,2,0,1:T(8,128)(2,1)} collective-permute-done((bf16[2,2,256,1024]{3,2,0,1:T(8,128)(2,1)S(1)}, bf16[2,2,256,1024]{3,2,0,1:T(8,128)(2,1)}, u32[]{:S(2)}, u32[]{:S(2)}) %collective-permute-start.1) | collective-permute-done | bytes 2097184 | tf_op jit(solution)/shard_map/ppermute | solution.py:14
  188.1 3.0 copy.55
  193.8 3.1 copy.53
  196.9 2.9 reshape_squeeze.9
  221.2 40.2 %all-gather.1 = bf16[32,1,128]{2,1,0:T(2,128)(2,1)S(1)} all-gather(bf16[1,1,128]{2,1,0:T(2,128)(2,1)} %bitcast.119), channel_id=1, replica_groups=mesh['grp'=4,'dev'=8] {'grp','dev'}, dimensions={0}, use_global_device_ids=true | all-gather | bytes 8448 | tf_op jit(solution)/shard_map/all_gather | solution.py:189
  262.0 5.9 convolution_add_fusion
  269.8 5.5 convolution_convert_fusion
  275.4 3.2 convolution_convert_fusion.4
  281.9 4.0 fusion.40
  285.9 35.7 %all-gather.14.cloned.1.call-done = bf16[4096,1024]{1,0:T(8,128)(2,1)} async-done(((bf16[128,1024]{1,0:T(8,128)(2,1)}), bf16[4096,1024]{1,0:T(8,128)(2,1)}) %all-gather.14.cloned.1.call-update) | async-done | bytes 8388624 | tf_op jit(solution)/shard_map/all_gather | solution.py:190
  321.6 8.2 %fusion.126 = (bf16[4096]{0:T(1024)(128)(2,1)}, bf16[256,4096]{1,0:T(8,128)(2,1)S(1)}) fusion(f32[256,4096]{1,0:T(8,128)} %copy-done.63, bf16[4096,1024]{1,0:T(8,128)(2,1)} %all-gather.14.cloned.1.call-done, bf16[256,1024]{1,0:T(8,128)(2,1)} %param.13, f32[256]{0:T(256)} %copy-done.41), kind=kOutput, calls=%fused_computation.212 | convolution fusion | flops 2169237504 | bytes 15213568 | tf_op jit(solution)/shard_map/re,fe->rf/dot_general | solution.py:243
  331.1 5.8 convolution_convert_fusion.1
  337.8 3.2 fusion.37
  347.1 5.8 stack.16
  352.9 3.9 multiply_reduce_fusion
  375.6 5.8 stack.15
  381.5 3.1 copy_dynamic-update-slice_fusion.1
  388.3 168.8 %collective-permute-done.2 = f32[2,2,256,1024]{2,3,1,0:T(8,128)S(1)} collective-permute-done((f32[2,2,256,1024]{2,3,1,0:T(8,128)S(1)}, f32[2,2,256,1024]{2,3,1,0:T(8,128)S(1)}, u32[]{:S(2)}, u32[]{:S(2)}) %collective-permute-start.2) | collective-permute-done | bytes 4194336 | tf_op jit(solution)/shard_map/ppermute | solution.py:14
  565.5 4.6 convolution_convert_fusion.2
  570.3 47.2 %reduce-scatter.9.cloned.1.call-done = bf16[128,4096]{1,0:T(8,128)(2,1)} async-done(((bf16[1024,4096]{1,0:T(8,128)(2,1)}), bf16[128,4096]{1,0:T(8,128)(2,1)}) %reduce-scatter.9.cloned.1.call-update) | async-done | bytes 1048592 | tf_op jit(solution)/shard_map/reduce_scatter | solution.py:304
  617.8 69.9 %reduce-scatter.5.cloned.1.call-done = bf16[128,3072]{1,0:T(8,128)(2,1)} async-done(((bf16[1024,3072]{1,0:T(8,128)(2,1)}), bf16[128,3072]{1,0:T(8,128)(2,1)}) %reduce-scatter.5.cloned.1.call-update) | async-done | bytes 786448 | tf_op jit(solution)/shard_map/reduce_scatter | solution.py:298
  689.7 7.5 convolution_add_fusion.2
  698.9 5.8 fusion.127
  704.7 5.1 fusion.75
  711.1 26.3 %all-reduce.8 = (bf16[1024]{0:T(1024)(128)(2,1)S(1)}, bf16[1024]{0:T(1024)(128)(2,1)S(1)}, bf16[4096]{0:T(1024)(128)(2,1)S(1)}, bf16[1024]{0:T(1024)(128)(2,1)S(1)}) all-reduce(bf16[1024]{0:T(1024)(128)(2,1)S(1)} %get-tuple-element.10, bf16[1024]{0:T(1024)(128)(2,1)S(1)} %get-tuple-element.13, ...), channel_id=3, replica_groups=mesh['grp'=4,'dev'=8] {'dev'}, use_global_device_ids=true, to_apply=%region_17.18.clone | all-reduce | flops 7168 | bytes 28672
  737.8 10.2 %all-reduce.9 = (bf16[128]{0:T(256)(128)(2,1)S(1)}, bf16[128]{0:T(256)(128)(2,1)S(1)}, bf16[512]{0:T(512)(128)(2,1)S(1)}, bf16[128]{0:T(256)(128)(2,1)S(1)}) all-reduce(bf16[128]{0:T(256)(128)(2,1)S(1)} %dynamic-slice.1, bf16[128]{0:T(256)(128)(2,1)S(1)} %dynamic-slice.3, ...), channel_id=1, replica_groups=mesh['grp'=4,'dev'=8] {'grp'}, use_global_device_ids=true, to_apply=%region_18.19 | all-reduce | flops 896 | bytes 3584 | tf_op jit(solution)/shard_map/psum | solution.py:318
  750.1 13.6 %all-reduce.13.cloned.1.call-done = (bf16[128,1024]{1,0:T(8,128)(2,1)}, bf16[128,4096]{1,0:T(8,128)(2,1)}, bf16[512,1024]{1,0:T(8,128)(2,1)}) async-done(((bf16[128,1024]{1,0:T(8,128)(2,1)}, bf16[128,4096]{1,0:T(8,128)(2,1)}, bf16[512,1024]{1,0:T(8,128)(2,1)}), (bf16[128,1024]{1,0:T(8,128)(2,1)}, bf16[128,4096]{1,0:T(8,128)(2,1)}, bf16[512,1024]{1,0:T(8,128)(2,1)})) %all-reduce.13.cloned.1.call-update) | async-done | bytes 2359312 | tf_op jit(solution)/shard_map/psum | solution.py:321
  765.6 2.8 convert_element_type.211
  769.9 39.3 %all-gather.16.cloned.1.call-done = bf16[512,3072]{1,0:T(8,128)(2,1)} async-done(((bf16[128,3072]{1,0:T(8,128)(2,1)}), bf16[512,3072]{1,0:T(8,128)(2,1)}) %all-gather.16.cloned.1.call-update) | async-done | bytes 3145744 | tf_op jit(solution)/shard_map/all_gather | solution.py:10
  (263 shorter events, 113.7 us)
Async XLA Ops:
  7.2 76.2 %all-gather.8.cloned.1.call-start = ((), (), s32[]{:S(2)}) async-start(), calls=%async_computation.4 | async-start | bytes 6488064 | tf_op jit(solution)/shard_map/all_gather | solution.py:186
  7.9 254.1 %all-gather.12.cloned.1.call-start = ((), (), s32[]{:S(2)}) async-start(), calls=%async_computation.6 | async-start | bytes 8650752 | tf_op jit(solution)/shard_map/all_gather | solution.py:188
  8.7 266.7 %all-gather.10.cloned.1.call-start = ((), (), s32[]{:S(2)}) async-start(), calls=%async_computation.5 | async-start | bytes 2162688 | tf_op jit(solution)/shard_map/all_gather | solution.py:187
  9.4 312.2 %all-gather.14.cloned.1.call-start = ((), (), s32[]{:S(2)}) async-start(), calls=%async_computation.7 | async-start | bytes 8650752 | tf_op jit(solution)/shard_map/all_gather | solution.py:190
  10.0 560.3 %reduce-scatter.7.cloned.1.call-start = ((), (), s32[]{:S(2)}) async-start(), calls=%async_computation.9 | async-start | bytes 2359296 | tf_op jit(solution)/shard_map/reduce_scatter | solution.py:301
  58.7 203.3 %copy-start.43 = (f32[256]{0:T(256)}, f32[256]{0:T(256)S(1)}, u32[]{:S(2)}) copy-start(f32[256]{0:T(256)S(1)} %broadcast_multiply_fusion.2) | copy-start | bytes 3076
  60.2 28.0 %copy-start.46 = (f32[256]{0:T(256)}, f32[256]{0:T(256)S(1)}, u32[]{:S(2)}) copy-start(f32[256]{0:T(256)S(1)} %add_rsqrt_fusion) | copy-start | bytes 3076
  92.2 7.9 copy-start.61
  92.2 11.1 %copy-start.59 = (s32[256]{0:T(256)S(1)}, s32[256]{0:T(256)}, u32[]{:S(2)}) copy-start(s32[256]{0:T(256)} %get-tuple-element.67) | copy-start | bytes 3076
  93.9 2.9 collective-permute-start
  98.6 84.4 %collective-permute-start.1 = (bf16[2,2,256,1024]{3,2,0,1:T(8,128)(2,1)S(1)}, bf16[2,2,256,1024]{3,2,0,1:T(8,128)(2,1)}, u32[]{:S(2)}, u32[]{:S(2)}) collective-permute-start(bf16[2,2,256,1024]{3,2,0,1:T(8,128)(2,1)S(1)} %maximum_select_fusion.1), channel_id=1, source_target_pairs={{0,2},{1,3},{2,0},{3,1},{4,6},{5,7},{6,4},{7,5},{8,10},{9,11},{10,... | collective-permute-start | bytes 6291464 | tf_op jit(solution)/shard_map/ppermute | solution.py:14
  102.6 172.8 %copy-start.41 = (f32[256]{0:T(256)}, f32[256]{0:T(256)S(1)}, u32[]{:S(2)}) copy-start(f32[256]{0:T(256)S(1)} %and_convert_fusion) | copy-start | bytes 3076
  202.0 9.7 %copy-start.8 = (f32[4,256,1024]{2,1,0:T(8,128)}, f32[4,256,1024]{2,1,0:T(8,128)S(1)}, u32[]{:S(2)}) copy-start(f32[4,256,1024]{2,1,0:T(8,128)S(1)} %get-tuple-element.49) | copy-start | bytes 12582916
  202.0 9.7 %copy-start.51 = (f32[4,256]{1,0:T(4,128)}, f32[4,256]{1,0:T(4,128)S(1)}, u32[]{:S(2)}) copy-start(f32[4,256]{1,0:T(4,128)S(1)} %get-tuple-element.48) | copy-start | bytes 12292
  206.2 8.6 %copy-start.3 = (f32[4,256,1024]{2,1,0:T(8,128)}, f32[4,256,1024]{2,1,0:T(8,128)S(1)}, u32[]{:S(2)}) copy-start(f32[4,256,1024]{2,1,0:T(8,128)S(1)} %get-tuple-element.51) | copy-start | bytes 12582916
  206.2 8.6 %copy-start.54 = (f32[4,256]{1,0:T(4,128)}, f32[4,256]{1,0:T(4,128)S(1)}, u32[]{:S(2)}) copy-start(f32[4,256]{1,0:T(4,128)S(1)} %get-tuple-element.50) | copy-start | bytes 12292
  207.3 7.5 copy-start.55
  218.0 43.9 %copy-start.11 = (bf16[256,1024]{1,0:T(8,128)(2,1)S(1)}, bf16[256,1024]{1,0:T(8,128)(2,1)}, u32[]{:S(2)}) copy-start(bf16[256,1024]{1,0:T(8,128)(2,1)} %param.12) | copy-start | bytes 1572868
  221.1 349.2 %reduce-scatter.11.cloned.1.call-start = ((), (), s32[]{:S(2)}) async-start(), calls=%async_computation.11 | async-start | bytes 9437184 | tf_op jit(solution)/shard_map/reduce_scatter | solution.py:310
  275.3 342.2 %reduce-scatter.9.cloned.1.call-start = ((), (), s32[]{:S(2)}) async-start(), calls=%async_computation.10 | async-start | bytes 9437184 | tf_op jit(solution)/shard_map/reduce_scatter | solution.py:304
  321.6 9.6 %copy-start.44 = (f32[256]{0:T(256)S(1)}, f32[256]{0:T(256)}, u32[]{:S(2)}) copy-start(f32[256]{0:T(256)} %copy-done.43) | copy-start | bytes 3076
  321.6 9.6 %copy-start.47 = (f32[256]{0:T(256)S(1)}, f32[256]{0:T(256)}, u32[]{:S(2)}) copy-start(f32[256]{0:T(256)} %copy-done.46) | copy-start | bytes 3076
  336.9 350.8 %reduce-scatter.5.cloned.1.call-start = ((), (), s32[]{:S(2)}) async-start(), calls=%async_computation.8 | async-start | bytes 7077888 | tf_op jit(solution)/shard_map/reduce_scatter | solution.py:298
  386.7 170.4 %collective-permute-start.2 = (f32[2,2,256,1024]{2,3,1,0:T(8,128)S(1)}, f32[2,2,256,1024]{2,3,1,0:T(8,128)S(1)}, u32[]{:S(2)}, u32[]{:S(2)}) collective-permute-start(f32[2,2,256,1024]{2,3,1,0:T(8,128)S(1)} %slice_select_fusion), channel_id=1, source_target_pairs={{0,2},{1,3},{2,0},{3,1},{4,6},{5,7},{6,4},{7,5},{8,10},{9,11},{10,... | collective-permute-start | bytes 12582920 | tf_op jit(solution)/shard_map/ppermute | solution.py:14
  558.2 6.2 collective-permute-start.3
  570.2 117.6 %copy-start.62 = (u32[32]{0:T(128)S(1)}, u32[32]{0:T(128)}, u32[]{:S(2)}) copy-start(u32[32]{0:T(128)} %constant.185) | copy-start | bytes 388
  570.2 119.5 %copy-start.60 = (bf16[1024]{0:T(1024)(128)(2,1)S(1)}, bf16[1024]{0:T(1024)(128)(2,1)}, u32[]{:S(2)}) copy-start(bf16[1024]{0:T(1024)(128)(2,1)} %get-tuple-element.14) | copy-start | bytes 6148
  570.2 193.5 %all-reduce.13.cloned.1.call-start = ((), (), s32[]{:S(2)}) async-start(), calls=%async_computation.13 | async-start | bytes 4718592 | tf_op jit(solution)/shard_map/psum | solution.py:321
  617.5 191.8 %all-gather.16.cloned.1.call-start = ((), (), s32[]{:S(2)}) async-start(), calls=%async_computation.12 | async-start | bytes 3932160 | tf_op jit(solution)/shard_map/all_gather | solution.py:10
  689.7 7.6 copy-start.21
  689.7 7.6 copy-start.29
  689.7 7.6 copy-start.42
  (46 other events, 146.1 us)
Sparse Core Ops, SparseCore 0:
  11.0 72.3 all-gather.7
  86.3 95.9 all-gather.11
  185.3 57.3 all-gather.9
  245.6 75.9 all-gather.13
  323.7 34.5 reduce-scatter.6
  360.4 144.0 reduce-scatter.10
  506.8 110.6 reduce-scatter.8
  619.8 67.8 reduce-scatter.4
  691.1 72.5 all-reduce.12
  765.4 43.8 all-gather.15
